TPU v7x, 512 devices: a whole 4x4x16 slice. The times are simulated.
512 devices in a mesh: fsdp: 32 (over y_lo, z), expert: 16 (over x, y_hi, core).
Axes of the slice: x: 4, y: 4 (y_hi: 2, y_lo: 2; y = y_hi * 2 + y_lo), z: 16, core: 2. Of those that a mesh axis runs over, the one named last changes fastest.
Arguments:
- tokens: bfloat16 [131072, 1440], P(('fsdp', 'expert')), may hold values from -6 to 6
- cotangent: bfloat16 [131072, 1440], P(('fsdp', 'expert')), may hold values from -6 to 6
- expert_ids: int32 [131072, 4], P(('fsdp', 'expert')), may hold values from 0 to 127, as said below
- gates: float32 [131072, 4], P(('fsdp', 'expert')), may hold values from 0.1 to 0.6
- gate_up_weight: bfloat16 [16, 1440, 2880], P('expert', 'fsdp'), may hold values from -0.15625 to 0.15625
- down_matrix: bfloat16 [16, 1440, 1440], P('expert', 'fsdp'), may hold values from -0.15625 to 0.15625
Outputs:
- output: bfloat16 [131072, 1440], P(('fsdp', 'expert'))
- input_grad: bfloat16 [131072, 1440], P(('fsdp', 'expert'))
Inputs may be any that keep to these rules, and one draw needn't show every extreme that they name: `expert_ids`: each row names 4 different experts.
All inputs are finite; a program needn't handle non-finite values.
Results may differ from a plain program's by a relative error of at most 0.006.
Values may be sent and summed in bfloat16 or wider, within the bound.
A program may use at most 128 MiB of HBM per device.

v0:
```python
import jax
import jax.numpy as jnp
from jax import lax
from jax.sharding import PartitionSpec as P

CAP = 16


def slot_places(expert_ids, window, slot_capacity):
    count = expert_ids.shape[0]
    choose = expert_ids.shape[1]
    flat = expert_ids.reshape(-1)
    onehot = (flat[:, None] == jnp.arange(window, dtype=jnp.int32)[None, :]).astype(jnp.int32)
    before = jnp.cumsum(onehot, axis=0) - onehot
    slot = jnp.sum(before * onehot, axis=1)
    kept = (flat < window) & (slot < slot_capacity)
    places = jnp.where(kept, flat * slot_capacity + slot, window * slot_capacity)
    return places.reshape(count, choose)


def shards(tokens, cotangent, expert_ids, gates, gate_up_weight, down_matrix):
    window = lax.axis_size("expert")
    width = tokens.shape[1]
    count = tokens.shape[0]
    choose = expert_ids.shape[1]
    hidden_width = down_matrix.shape[1] * lax.axis_size("fsdp")
    places = slot_places(expert_ids, window, CAP)
    pairs = count * choose
    source = (
        jnp.full((window * CAP + 1,), pairs, jnp.int32)
        .at[places.reshape(-1)]
        .set(jnp.arange(pairs, dtype=jnp.int32))[:-1]
    )
    token_index = source // choose
    zero_row = jnp.zeros((1, width), jnp.bfloat16)
    padded_tokens = jnp.concatenate([tokens, zero_row], axis=0)
    padded_cotangent = jnp.concatenate([cotangent, zero_row], axis=0)
    slot_gate = jnp.concatenate([gates.reshape(-1), jnp.zeros((1,), jnp.float32)], axis=0)[source]
    along_cols = (((1,), (1,)), ((), ()))
    send_rows = padded_tokens[token_index].reshape(window, CAP, width)
    send_grads = (
        (padded_cotangent[token_index].astype(jnp.float32) * slot_gate[:, None])
        .astype(jnp.bfloat16)
        .reshape(window, CAP, width)
    )
    rows_in = lax.all_to_all(send_rows, "expert", split_axis=0, concat_axis=0, tiled=True)
    rows_in = rows_in.reshape(window * CAP, width)
    full_gate_up, full_down = (
        lax.all_gather(gate_up_weight, "fsdp", axis=1, tiled=True),
        lax.all_gather(down_matrix, "fsdp", axis=1, tiled=True),
    )
    gate_up_matrix = full_gate_up[0]
    down = full_down[0]
    pre = jnp.dot(rows_in, gate_up_matrix, preferred_element_type=jnp.float32)
    act = pre[:, :hidden_width]
    upper = pre[:, hidden_width:]
    sigma = jax.nn.sigmoid(act)
    hidden = (act * sigma * upper).astype(jnp.bfloat16)
    grad_in = lax.all_to_all(send_grads, "expert", split_axis=0, concat_axis=0, tiled=True)
    grad_in = grad_in.reshape(window * CAP, width)
    expert_out = jnp.dot(hidden, down, preferred_element_type=jnp.float32).astype(jnp.bfloat16)
    hidden_grad = lax.dot_general(grad_in, down, along_cols, preferred_element_type=jnp.float32)
    expert_out = expert_out.reshape(window, CAP, width)
    out_back = lax.all_to_all(expert_out, "expert", split_axis=0, concat_axis=0, tiled=True)
    pre_grad = jnp.concatenate(
        [hidden_grad * upper * sigma * (1.0 + act * (1.0 - sigma)), hidden_grad * act * sigma],
        axis=1,
    ).astype(jnp.bfloat16)
    row_grads = (
        lax.dot_general(pre_grad, gate_up_matrix, along_cols, preferred_element_type=jnp.float32)
        .astype(jnp.bfloat16)
        .reshape(window, CAP, width)
    )
    grads_back = lax.all_to_all(row_grads, "expert", split_axis=0, concat_axis=0, tiled=True)
    out_flat = jnp.concatenate([out_back.reshape(window * CAP, width), zero_row], axis=0)
    grads_flat = jnp.concatenate([grads_back.reshape(window * CAP, width), zero_row], axis=0)
    out_rows = out_flat[places].astype(jnp.float32)
    back_rows = grads_flat[places].astype(jnp.float32)
    output = jnp.sum(gates[:, :, None] * out_rows, axis=1)
    input_grad = jnp.sum(back_rows, axis=1)
    return (output.astype(jnp.bfloat16), input_grad.astype(jnp.bfloat16))


def solution(mesh):
    in_specs = (
        P(("fsdp", "expert"), None),
        P(("fsdp", "expert"), None),
        P(("fsdp", "expert"), None),
        P(("fsdp", "expert"), None),
        P("expert", "fsdp", None),
        P("expert", "fsdp", None),
    )
    out_specs = (P(("fsdp", "expert"), None), P(("fsdp", "expert"), None))
    return jax.shard_map(shards, mesh=mesh, in_specs=in_specs, out_specs=out_specs, check_vma=False)
```

profile of v0, /device:TPU:1, one launch (start us, length us, event | category | flops | bytes accessed | tf_op | source)
XLA Modules:
  0.0 464.0 jit_solution(13671796928818410698)
XLA Ops:
  7.2 2.2 copy.51
  12.5 4.5 reduce-window.6
  18.3 4.3 scatter_custom_fusion
  24.8 10.4 %all-to-all-start = ((bf16[16,16,1440]{2,1,0:T(8,128)(2,1)}), bf16[16,16,1440]{2,1,0:T(8,128)(2,1)S(1)}, u32[]{:S(2)}, u32[]{:S(2)}) async-start(bf16[16,16,1440]{2,1,0:T(8,128)(2,1)} %bitcast.4), calls=%async_computation | async-start | bytes 1572864 | tf_op jit(solution)/shard_map/all_to_all | solution.py:46
  40.0 184.0 %all-to-all-done = bf16[16,16,1440]{2,1,0:T(8,128)(2,1)S(1)} async-done(((bf16[16,16,1440]{2,1,0:T(8,128)(2,1)}), bf16[16,16,1440]{2,1,0:T(8,128)(2,1)S(1)}, u32[]{:S(2)}, u32[]{:S(2)}) %all-to-all-start) | async-done | bytes 737312 | tf_op jit(solution)/shard_map/all_to_all | solution.py:46
  224.0 4.7 %all-to-all-start.2 = ((bf16[16,16,1440]{2,1,0:T(8,128)(2,1)}), bf16[16,16,1440]{2,1,0:T(8,128)(2,1)S(1)}, u32[]{:S(2)}, u32[]{:S(2)}) async-start(bf16[16,16,1440]{2,1,0:T(8,128)(2,1)} %fusion.18), calls=%async_computation.2 | async-start | bytes 1572864 | tf_op jit(solution)/shard_map/all_to_all | solution.py:59
  228.7 11.2 %fusion.2 = f32[256,2880]{0,1:T(8,128)} fusion(bf16[256,1440]{1,0:T(8,128)(2,1)S(1)} %bitcast.51, bf16[1,1440,2880]{2,0,1:T(2,128)(2,1)} %all-gather.3.cloned.1.call-done), kind=kOutput, calls=%fused_computation.8 | convolution fusion | flops 2123366400 | bytes 11980800 | tf_op jit(solution)/shard_map/dot_general | solution.py:54
  239.9 5.1 %all-to-all-done.2 = bf16[16,16,1440]{2,1,0:T(8,128)(2,1)S(1)} async-done(((bf16[16,16,1440]{2,1,0:T(8,128)(2,1)}), bf16[16,16,1440]{2,1,0:T(8,128)(2,1)S(1)}, u32[]{:S(2)}, u32[]{:S(2)}) %all-to-all-start.2) | async-done | bytes 737312 | tf_op jit(solution)/shard_map/all_to_all | solution.py:59
  245.0 103.0 %all-gather.5.cloned.1.call-done = bf16[1,1440,1440]{2,0,1:T(2,128)(2,1)} async-done(((bf16[1,45,1440]{2,0,1:T(2,128)(2,1)}), bf16[1,1440,1440]{2,0,1:T(2,128)(2,1)}) %all-gather.5.cloned.1.call-update) | async-done | bytes 4147216 | tf_op jit(solution)/shard_map/all_gather | solution.py:50
  348.1 6.2 %multiply_convert_fusion.1 = (bf16[256,1440]{0,1:T(8,128)(2,1)S(1)}, bf16[256,1440]{0,1:T(8,128)(2,1)S(1)}) fusion(f32[256,2880]{0,1:T(8,128)} %fusion.2, bf16[256,1440]{1,0:T(8,128)(2,1)S(1)} %bitcast.52, bf16[1,1440,1440]{2,0,1:T(2,128)(2,1)} %all-gather.5.cloned.1.call-done), kind=kOutput, calls=%fused_computation.27 | convolution fusion | flops 1066475520 | bytes 9308160 | tf_op jit(solution)/shard_map/dot_general | solution.py:62
  354.3 3.0 copy-done.4
  357.3 2.5 fusion.13
  360.9 24.4 %all-to-all-start.3 = ((bf16[16,16,1440]{2,1,0:T(8,128)(2,1)}), bf16[16,16,1440]{2,1,0:T(8,128)(2,1)S(1)}, u32[]{:S(2)}, u32[]{:S(2)}) async-start(bf16[16,16,1440]{2,1,0:T(8,128)(2,1)} %bitcast.10), calls=%async_computation.3 | async-start | bytes 1572864 | tf_op jit(solution)/shard_map/all_to_all | solution.py:74
  385.3 6.4 %fusion.10 = bf16[256,1440]{0,1:T(8,128)(2,1)S(1)} fusion(bf16[1,1440,1440]{2,0,1:T(2,128)(2,1)} %all-gather.5.cloned.1.call-done, f32[256,2880]{0,1:T(8,128)} %fusion.2), kind=kOutput, calls=%fused_computation.17 | convolution fusion | flops 1064263680 | bytes 7833600 | tf_op jit(solution)/shard_map/dot_general | solution.py:61
  392.9 6.6 %all-to-all-done.3 = bf16[16,16,1440]{2,1,0:T(8,128)(2,1)S(1)} async-done(((bf16[16,16,1440]{2,1,0:T(8,128)(2,1)}), bf16[16,16,1440]{2,1,0:T(8,128)(2,1)S(1)}, u32[]{:S(2)}, u32[]{:S(2)}) %all-to-all-start.3) | async-done | bytes 737312 | tf_op jit(solution)/shard_map/all_to_all | solution.py:74
  399.5 4.5 all-to-all-start.1
  404.2 14.1 %all-to-all-done.1 = bf16[16,16,1440]{2,1,0:T(8,128)(2,1)S(1)} async-done(((bf16[16,16,1440]{2,1,0:T(8,128)(2,1)}), bf16[16,16,1440]{2,1,0:T(8,128)(2,1)S(1)}, u32[]{:S(2)}, u32[]{:S(2)}) %all-to-all-start.1) | async-done | bytes 737312 | tf_op jit(solution)/shard_map/all_to_all | solution.py:64
  418.3 5.6 %gather_fusion.1 = bf16[1024,1440]{1,0:T(8,128)(2,1)} fusion(bf16[257,1440]{1,0:T(8,128)(2,1)S(1)} %concatenate.20, s32[1024]{0:T(1024)S(1)} %broadcast_clamp_fusion), kind=kCustom, calls=%fused_computation.1 | custom fusion | bytes 5902336 | tf_op jit(solution)/shard_map/gather | solution.py:77
  424.0 5.6 %gather_fusion.4 = bf16[1024,1440]{1,0:T(8,128)(2,1)} fusion(bf16[257,1440]{1,0:T(8,128)(2,1)S(1)} %concatenate.24, s32[1024]{0:T(1024)S(1)} %broadcast_clamp_fusion), kind=kCustom, calls=%fused_computation.4 | custom fusion | bytes 5902336 | tf_op jit(solution)/shard_map/gather | solution.py:78
  429.6 6.1 %reshape.154 = bf16[256,4,1440]{2,1,0:T(4,128)(2,1)} reshape(bf16[1024,1440]{1,0:T(8,128)(2,1)} %gather_fusion.4) | data formatting | bytes 5898240 | tf_op jit(solution)/shard_map/gather | solution.py:78
  435.7 6.8 %reduce_sum.38 = bf16[256,1440]{1,0:T(8,128)(2,1)} reduce(bf16[256,4,1440]{2,1,0:T(4,128)(2,1)} %reshape.154, bf16[]{:T(256)} %constant.14.clone.1), dimensions={1}, to_apply=%region_5.6 | reduce | flops 1105920 | bytes 3686402 | tf_op jit(solution)/shard_map/reduce_sum | solution.py:80
  442.5 2.3 copy.58
  444.8 3.8 reshape.172
  448.6 7.4 %multiply_reduce_fusion = bf16[256,1440]{1,0:T(8,128)(2,1)S(1)} fusion(f32[256,4,1440]{2,1,0:T(4,128)} %reshape.172, f32[256,4]{1,0:T(8,128)S(1)} %copy.43), kind=kLoop, calls=%fused_computation.10 | loop fusion | flops 2580480 | bytes 6639616 | tf_op jit(solution)/shard_map/reduce_sum | solution.py:79
  (53 shorter events, 14.9 us)
Async XLA Ops:
  7.2 10.7 %copy-start.1 = (bf16[256,1440]{0,1:T(8,128)(2,1)S(1)}, bf16[256,1440]{0,1:T(8,128)(2,1)}, u32[]{:S(2)}) copy-start(bf16[256,1440]{0,1:T(8,128)(2,1)} %param.6) | copy-start | bytes 2211844
  7.2 221.5 %all-gather.3.cloned.1.call-start = ((), (), s32[]{:S(2)}) async-start(), calls=%async_computation.4 | async-start | bytes 17487360 | tf_op jit(solution)/shard_map/all_gather | solution.py:49
  9.5 338.6 %all-gather.5.cloned.1.call-start = ((), (), s32[]{:S(2)}) async-start(), calls=%async_computation.5 | async-start | bytes 9123840 | tf_op jit(solution)/shard_map/all_gather | solution.py:50
  22.6 12.6 %copy-start.3 = (f32[256,4]{0,1:T(4,128)S(1)}, f32[256,4]{0,1:T(4,128)}, u32[]{:S(2)}) copy-start(f32[256,4]{0,1:T(4,128)} %param.9) | copy-start | bytes 12292
  24.8 12.5 %copy-start.2 = (bf16[256,1440]{0,1:T(8,128)(2,1)S(1)}, bf16[256,1440]{0,1:T(8,128)(2,1)}, u32[]{:S(2)}) copy-start(bf16[256,1440]{0,1:T(8,128)(2,1)} %param.7) | copy-start | bytes 2211844
  24.8 199.2 %all-to-all-start = ((bf16[16,16,1440]{2,1,0:T(8,128)(2,1)}), bf16[16,16,1440]{2,1,0:T(8,128)(2,1)S(1)}, u32[]{:S(2)}, u32[]{:S(2)}) async-start(bf16[16,16,1440]{2,1,0:T(8,128)(2,1)} %bitcast.4), calls=%async_computation | async-start | bytes 1572864 | tf_op jit(solution)/shard_map/all_to_all | solution.py:46
  224.0 21.0 %all-to-all-start.2 = ((bf16[16,16,1440]{2,1,0:T(8,128)(2,1)}), bf16[16,16,1440]{2,1,0:T(8,128)(2,1)S(1)}, u32[]{:S(2)}, u32[]{:S(2)}) async-start(bf16[16,16,1440]{2,1,0:T(8,128)(2,1)} %fusion.18), calls=%async_computation.2 | async-start | bytes 1572864 | tf_op jit(solution)/shard_map/all_to_all | solution.py:59
  348.1 9.2 %copy-start.4 = (bf16[1,1440,2880]{2,0,1:T(2,128)(2,1)S(1)}, bf16[1,1440,2880]{2,0,1:T(2,128)(2,1)}, u32[]{:S(2)}) copy-start(bf16[1,1440,2880]{2,0,1:T(2,128)(2,1)} %all-gather.3.cloned.1.call-done) | copy-start | bytes 24883204
  360.9 38.6 %all-to-all-start.3 = ((bf16[16,16,1440]{2,1,0:T(8,128)(2,1)}), bf16[16,16,1440]{2,1,0:T(8,128)(2,1)S(1)}, u32[]{:S(2)}, u32[]{:S(2)}) async-start(bf16[16,16,1440]{2,1,0:T(8,128)(2,1)} %bitcast.10), calls=%async_computation.3 | async-start | bytes 1572864 | tf_op jit(solution)/shard_map/all_to_all | solution.py:74
  399.5 18.8 %all-to-all-start.1 = ((bf16[16,16,1440]{2,1,0:T(8,128)(2,1)}), bf16[16,16,1440]{2,1,0:T(8,128)(2,1)S(1)}, u32[]{:S(2)}, u32[]{:S(2)}) async-start(bf16[16,16,1440]{2,1,0:T(8,128)(2,1)} %bitcast.6), calls=%async_computation.1 | async-start | bytes 1572864 | tf_op jit(solution)/shard_map/all_to_all | solution.py:64
  435.7 9.1 %copy-start = (bf16[1024,1440]{1,0:T(8,128)(2,1)S(1)}, bf16[1024,1440]{1,0:T(8,128)(2,1)}, u32[]{:S(2)}) copy-start(bf16[1024,1440]{1,0:T(8,128)(2,1)} %gather_fusion.1) | copy-start | bytes 8847364
Sparse Core Ops, SparseCore 0:
  10.7 211.0 all-gather.2
  224.4 123.6 all-gather.4
where the time goes:
time: 465 us; the launch traced here: 464 us
  waiting for transfers between devices  313 us (67%)
  local copies, waits for them, and re-layouts  46.4 us (10%)
  starting transfers between devices  44.1 us (9%)
  matrix products  26.3 us (6%)
  other arithmetic  20.1 us (4%)
  between operations  14.3 us (3%)
    all_to_all x1, waiting for transfers between devices, shards(): lax.all_to_all(send_rows, 'expert', split_axis=0, concat_axis=0, tiled=True)  184 us
    all_gather x1, waiting for transfers between devices, shards(): lax.all_gather(down_matrix, 'fsdp', axis=1, tiled=True)  103 us
    all_to_all x1, starting transfers between devices, shards(): lax.all_to_all(row_grads, 'expert', split_axis=0, concat_axis=0, tiled=True)  24.4 us
    all_to_all x1, waiting for transfers between devices, shards(): lax.all_to_all(expert_out, 'expert', split_axis=0, concat_axis=0, tiled=T...  14.1 us
    unnamed x18, local copies, waits for them, and re-layouts  11.9 us
    gather x2, local copies, waits for them, and re-layouts, shards(): back_rows = grads_flat[places].astype(jnp.float32)  11.8 us
    dot_general x1, matrix products, shards(): pre = jnp.dot(rows_in, gate_up_matrix, preferred_element_type=jnp.float32)  11.2 us
    all_to_all x1, starting transfers between devices, shards(): lax.all_to_all(send_rows, 'expert', split_axis=0, concat_axis=0, tiled=True)  10.4 us
  transfers between devices with their start and end apart: 6, of which 5 were waited for; matrix products, arithmetic and copies ran while one was open for 8% of the time, Pallas kernels for 0%

commit v1 on v0

v1 whole, which is shorter than its diff:
```python
import functools

import jax
import jax.numpy as jnp
import numpy as np
from jax import lax
from jax.experimental import pallas as pl
from jax.experimental.pallas import tpu as pltpu
from jax.sharding import PartitionSpec as P

MESH = pl.DeviceIdType.MESH
CAP = 16
LANE = 128
BF = jnp.bfloat16
F32 = jnp.float32
NN = (((1,), (0,)), ((), ()))
NT = (((1,), (1,)), ((), ()))


def dot(a, b, dims=NN):
    return lax.dot_general(a, b, dims, preferred_element_type=F32)


def onehot(mask):
    return jnp.where(mask, 1.0, 0.0).astype(BF)


def layer_kernel(
    cfg,
    gate_up_hbm, down_hbm, tok_hbm, cot_hbm, ids_ref, gates_ref, place_ref,
    out_ref, igrad_ref,
    gu_own, dn_own, own32, own_gu, own_dn,
    w_gate, w_up, w_down,
    tok, cot, rows_nat, rows_send, rows_in, grads_send, grads_in,
    hid, fac_gate, fac_up, pg_gate, pg_up,
    out_send, rg_send, out_recv, rg_recv,
    pick, pick_t, mix_hi, mix_lo,
    in_sem, swap_send, swap_recv, ring_send_sem, ring_recv_sem, last_send_sem, last_recv_sem,
    sib_send_sem, sib_recv_sem, a2a_send_sem, a2a_recv_sem,
):
    nz, ne, per, pad, width = cfg["nz"], cfg["ne"], cfg["per"], cfg["pad"], cfg["width"]
    dp = 2 * nz * pad
    chunks = w_down.shape[0]
    cw = w_down.shape[2]
    tile = cfg["tile"]
    rows = ne * CAP
    toks = ids_ref.shape[1]
    kb = nz // 2 - 1

    f = lax.axis_index("fsdp")
    e = lax.axis_index("expert")
    ylo = lax.div(f, nz)
    z = lax.rem(f, nz)
    c = lax.rem(e, 2)
    e2 = lax.div(e, 2)
    keeps = ylo == c
    swaps = ylo != c

    barrier = pltpu.get_barrier_semaphore()

    def greet(i, _):
        gf = lax.div(i, ne) * nz + z
        ge = lax.rem(i, ne)

        @pl.when((gf != f) | (ge != e))
        def _():
            pl.semaphore_signal(barrier, inc=1, device_id=(gf, ge), device_id_type=MESH)

        return 0

    znext = ylo * nz + lax.rem(z + 1, nz)
    zprev = ylo * nz + lax.rem(z + nz - 1, nz)
    pl.semaphore_signal(barrier, inc=1, device_id=(znext, e), device_id_type=MESH)
    pl.semaphore_signal(barrier, inc=1, device_id=(zprev, e), device_id_type=MESH)
    lax.fori_loop(0, 2 * ne, greet, 0)

    load_gu = pltpu.make_async_copy(gate_up_hbm, gu_own, in_sem.at[0])
    load_dn = pltpu.make_async_copy(down_hbm, dn_own, in_sem.at[1])
    load_tok = pltpu.make_async_copy(tok_hbm, tok.at[pl.ds(0, width)], in_sem.at[2])
    load_cot = pltpu.make_async_copy(cot_hbm, cot.at[pl.ds(0, width)], in_sem.at[3])
    load_gu.start()
    load_dn.start()
    load_tok.start()
    load_cot.start()

    def spans(base, j):
        p = np.arange(LANE * j, LANE * (j + 1))
        p = p[p % pad < per]
        d = per * (p // pad) + p % pad + base
        start = int(d.min()) // LANE * LANE
        assert d.max() < start + 2 * LANE
        return start

    own32[...] = jnp.zeros_like(own32)
    load_gu.wait()
    for half in range(2):
        for j in range(dp // LANE):
            start = spans(half * width, j)
            depth = min(2 * LANE, 2 * width - start)
            hid_id = lax.broadcasted_iota(jnp.int32, (depth, LANE), 0) + (start - half * width)
            sel = onehot(hid_id == place_ref[0:1, LANE * j : LANE * (j + 1)])
            own32[0:per, LANE * j : LANE * (j + 1)] = dot(gu_own[:, start : start + depth], sel)
        own_gu[half] = own32[...].astype(BF)
    load_dn.wait()
    own32[...] = jnp.zeros_like(own32)
    own32[0:per, 0:width] = dn_own[...].astype(F32)
    for n in range(chunks):
        own_dn[n] = own32[:, cw * n : cw * (n + 1)].astype(BF)

    weights = [w_gate, w_up] + [w_down.at[n] for n in range(chunks)]
    owns = [own_gu.at[0], own_gu.at[1]] + [own_dn.at[n] for n in range(chunks)]

    def block(p, core, b):
        return weights[p].at[pl.ds(pl.multiple_of((core * nz + b) * pad, 16), pad)]

    def wait_for(ref, sem):
        pltpu.make_async_copy(ref, ref, sem).wait()

    def start_swap(p):
        @pl.when(keeps)
        def _():
            pltpu.make_async_copy(owns[p], block(p, c, z), swap_recv.at[p]).start()

        @pl.when(swaps)
        def _():
            pltpu.make_async_remote_copy(
                src_ref=owns[p], dst_ref=block(p, 1 - c, z),
                send_sem=swap_send.at[p], recv_sem=swap_recv.at[p],
                device_id=((1 - ylo) * nz + z, e2 * 2 + 1 - c), device_id_type=MESH,
            ).start()

    def ring_send(p, way, k):
        b = lax.rem(z + nz - k, nz) if way == 0 else lax.rem(z + k, nz)
        pltpu.make_async_remote_copy(
            src_ref=block(p, c, b), dst_ref=block(p, c, b),
            send_sem=ring_send_sem.at[p, way], recv_sem=ring_recv_sem.at[p, way, k],
            device_id=(znext if way == 0 else zprev, e), device_id_type=MESH,
        ).start()

    def last_send(p):
        b = lax.rem(z + nz - (1 - 2 * c) * kb, nz)
        pltpu.make_async_remote_copy(
            src_ref=block(p, c, b), dst_ref=block(p, c, b),
            send_sem=last_send_sem.at[p], recv_sem=last_recv_sem.at[p],
            device_id=(ylo * nz + lax.rem(z + nz + 1 - 2 * c, nz), e), device_id_type=MESH,
        ).start()

    def sib_send(p, b):
        pltpu.make_async_remote_copy(
            src_ref=block(p, c, b), dst_ref=block(p, c, b),
            send_sem=sib_send_sem.at[p], recv_sem=sib_recv_sem.at[p],
            device_id=(f, e2 * 2 + 1 - c), device_id_type=MESH,
        ).start()

    def ring_open(p):
        wait_for(block(p, c, z), swap_recv.at[p])
        ring_send(p, 0, 0)
        ring_send(p, 1, 0)
        sib_send(p, z)

    def ring_step(p, k):
        came = (lax.rem(z + nz - 1 - k, nz), lax.rem(z + 1 + k, nz))
        for way in range(2):
            wait_for(block(p, c, came[way]), ring_recv_sem.at[p, way, k])
            if k < kb - 1:
                ring_send(p, way, k + 1)
            sib_send(p, came[way])
        if k == kb - 1:
            last_send(p)

    def ring_close(p):
        b = lax.rem(z + nz // 2, nz)
        wait_for(block(p, c, b), last_recv_sem.at[p])
        sib_send(p, b)

    def ring_here(p):
        wait_for(weights[p].at[pl.ds(pl.multiple_of((1 - c) * nz * pad, 16), nz * pad)], sib_recv_sem.at[p])

    def go(i, src, dst, gf, ge, place):
        @pl.when((gf != f) | (ge != e))
        def _():
            pltpu.make_async_remote_copy(
                src_ref=src, dst_ref=dst, send_sem=a2a_send_sem.at[i], recv_sem=a2a_recv_sem.at[i],
                device_id=(gf, ge), device_id_type=MESH,
            ).start()

        @pl.when((gf == f) & (ge == e))
        def _():
            pltpu.make_async_copy(src, dst, a2a_recv_sem.at[i]).start()

    def sixteen(ref, i):
        return ref.at[pl.ds(pl.multiple_of(i * CAP, CAP), CAP)]

    def send_out(i, src, dst):
        def one(t, _):
            x = lax.rem(e + t, ne)
            go(i, sixteen(src, x), sixteen(dst, e), lax.rem(x, 2) * nz + z, lax.div(x, 2) * 2 + ylo, x)
            return 0

        lax.fori_loop(0, ne, one, 0)

    def send_back(i, src, dst):
        def one(t, _):
            x = lax.rem(e + t, ne)
            go(i, sixteen(src, x), sixteen(dst, e2 * 2 + ylo), c * nz + z, x, x)
            return 0

        lax.fori_loop(0, ne, one, 0)

    def sent(i, src):
        @pl.when(keeps)
        def _():
            wait_for(src.at[pl.ds(0, rows - CAP)], a2a_send_sem.at[i])

        @pl.when(swaps)
        def _():
            wait_for(src, a2a_send_sem.at[i])

    def make_slots():
        ci = lax.broadcasted_iota(jnp.int32, (rows, toks), 0)
        expert = lax.shift_right_logical(ci, 4)
        hit = jnp.zeros((rows, toks), F32)
        gate = jnp.zeros((rows, toks), F32)
        for k in range(ids_ref.shape[0]):
            same = ids_ref[k : k + 1, :] == expert
            hit = jnp.where(same, 1.0, hit)
            gate = jnp.where(same, gates_ref[k : k + 1, :], gate)
        earlier = onehot(
            lax.broadcasted_iota(jnp.int32, (toks, toks), 0) < lax.broadcasted_iota(jnp.int32, (toks, toks), 1)
        )
        slot = dot(hit.astype(BF), earlier)
        want = jnp.bitwise_and(ci, CAP - 1).astype(F32)
        kept = jnp.where(slot == want, hit, 0.0)
        gate = gate * kept
        pick[...] = kept.astype(BF)
        pick_t[...] = kept.T.astype(BF)
        mixed = gate.T
        high = mixed.astype(BF)
        mix_hi[...] = high
        mix_lo[...] = (mixed - high.astype(F32)).astype(BF)
        return jnp.sum(gate, axis=1, keepdims=True)

    def columns(n):
        return slice(tile * n, tile * (n + 1))

    def make_rows():
        load_tok.wait()
        for n in range(dp // tile):
            rows_nat[:, columns(n)] = dot(pick[...], tok[columns(n), :], NT).astype(BF)
        for j in range(dp // LANE):
            start = spans(0, j)
            depth = min(2 * LANE, dp - start)
            d = lax.broadcasted_iota(jnp.int32, (depth, LANE), 0) + start
            sel = onehot(d == place_ref[0:1, LANE * j : LANE * (j + 1)])
            rows_send[:, LANE * j : LANE * (j + 1)] = dot(rows_nat[:, start : start + depth], sel).astype(BF)

    def make_grads(slot_gate):
        load_cot.wait()
        for n in range(dp // tile):
            grads_send[:, columns(n)] = (dot(pick[...], cot[columns(n), :], NT) * slot_gate).astype(BF)

    def forward_tile(n):
        act = dot(rows_in[...], w_gate[:, columns(n)])
        upper = dot(rows_in[...], w_up[:, columns(n)])
        sigma = jax.nn.sigmoid(act)
        gated = act * sigma
        hid[:, columns(n)] = (gated * upper).astype(BF)
        fac_gate[:, columns(n)] = upper * sigma * (1.0 + act * (1.0 - sigma))
        fac_up[:, columns(n)] = gated

    def backward_tile(n):
        grad = dot(grads_in[:, 0:cw], w_down[0, columns(n), :], NT)
        for m in range(1, chunks):
            grad = grad + dot(grads_in[:, cw * m : cw * (m + 1)], w_down[m, columns(n), :], NT)
        pg_gate[:, columns(n)] = (grad * fac_gate[:, columns(n)]).astype(BF)
        pg_up[:, columns(n)] = (grad * fac_up[:, columns(n)]).astype(BF)

    tok[width:dp, :] = jnp.zeros((dp - width, toks), BF)
    cot[width:dp, :] = jnp.zeros((dp - width, toks), BF)

    pl.semaphore_wait(barrier, 2 * ne + 1)

    first, second = [0, 1], list(range(2, 2 + chunks))
    for p in first + second:
        start_swap(p)
    for p in first:
        ring_open(p)
    slot_gate = make_slots()
    make_rows()
    send_out(0, rows_send, rows_in)
    for p in first:
        ring_step(p, 0)
    make_grads(slot_gate)
    send_out(1, grads_send, grads_in)
    for k in range(1, kb):
        for p in first:
            ring_step(p, k)
    for p in second:
        ring_open(p)
    for p in first:
        ring_close(p)
    for p in first:
        ring_here(p)
    wait_for(rows_in, a2a_recv_sem.at[0])
    tiles = dp // tile
    done = 0
    for k in range(kb):
        for p in second:
            ring_step(p, k)
        upto = tiles if k == kb - 1 else min(tiles, k + 1)
        for n in range(done, upto):
            forward_tile(n)
        done = upto
    for p in second:
        ring_close(p)
    wait_for(grads_in, a2a_recv_sem.at[1])
    for n in range(chunks):
        ring_here(2 + n)
        out_send[n] = dot(hid[...], w_down[n]).astype(BF)
        send_back(2 + n, out_send.at[n], out_recv.at[n])
    for n in range(tiles):
        backward_tile(n)
    for n in range(chunks):
        for m in range(cw // tile):
            here = slice(cw * n + tile * m, cw * n + tile * (m + 1))
            rg_send[n, :, columns(m)] = (
                dot(pg_gate[...], w_gate[here, :], NT) + dot(pg_up[...], w_up[here, :], NT)
            ).astype(BF)
        send_back(2 + chunks + n, rg_send.at[n], rg_recv.at[n])

    eye = onehot(
        lax.broadcasted_iota(jnp.int32, (LANE, LANE), 0) == lax.broadcasted_iota(jnp.int32, (LANE, LANE), 1)
    )
    for n in range(chunks):
        wait_for(out_recv.at[n], a2a_recv_sem.at[2 + n])
        total = (dot(mix_hi[...], out_recv[n]) + dot(mix_lo[...], out_recv[n])).astype(BF)
        for m in range(cw // LANE):
            d = cw * n + LANE * m
            size = min(LANE, width - d)
            if size > 0:
                turned = dot(eye, total[:, LANE * m : LANE * (m + 1)], NT).astype(BF)
                out_ref[d : d + size, :] = turned[0:size, :]
    for n in range(chunks):
        wait_for(rg_recv.at[n], a2a_recv_sem.at[2 + chunks + n])
        rows_nat[:, cw * n : cw * (n + 1)] = dot(pick_t[...], rg_recv[n]).astype(BF)
    for j in range(pl.cdiv(width, LANE)):
        d = np.arange(LANE * j, min(width, LANE * (j + 1)))
        p = pad * (d // per) + d % per
        start = int(p.min()) // LANE * LANE
        stop = (int(p.max()) // LANE + 1) * LANE
        di = lax.broadcasted_iota(jnp.int32, (LANE, stop - start), 0) + LANE * j
        sel = onehot(di == place_ref[0:1, start:stop])
        turned = dot(sel, rows_nat[:, start:stop], NT).astype(BF)
        igrad_ref[LANE * j : LANE * j + len(d), :] = turned[0 : len(d), :]

    for p in first + second:
        for way in range(2):
            wait_for(weights[p].at[pl.ds(0, kb * pad)], ring_send_sem.at[p, way])
        wait_for(weights[p].at[pl.ds(0, pad)], last_send_sem.at[p])
        wait_for(weights[p].at[pl.ds(0, nz * pad)], sib_send_sem.at[p])

        @pl.when(swaps)
        def _():
            wait_for(owns[p], swap_send.at[p])

    sent(0, rows_send)
    sent(1, grads_send)
    for n in range(chunks):
        sent(2 + n, out_send.at[n])
        sent(2 + chunks + n, rg_send.at[n])


def shards(mesh_shape, tokens, cotangent, expert_ids, gates, gate_up_weight, down_matrix):
    ne = mesh_shape["expert"]
    nz = mesh_shape["fsdp"] // 2
    toks, width = tokens.shape
    per = down_matrix.shape[1]
    pad = pl.cdiv(per, 16) * 16
    dp = 2 * nz * pad
    chunks = 3
    cw = dp // chunks
    tile = 256 if cw % 256 == 0 else 128
    rows = ne * CAP
    pieces = 2 + chunks
    p = np.arange(dp)
    place = np.where(p % pad < per, per * (p // pad) + p % pad, -(1 << 20)).astype(np.int32)[None]
    cfg = dict(nz=nz, ne=ne, per=per, pad=pad, width=width, tile=tile)
    any_spec = pl.BlockSpec(memory_space=pl.ANY)
    vmem_spec = pl.BlockSpec(memory_space=pltpu.VMEM)
    dma = pltpu.SemaphoreType.DMA
    flat = (rows, dp)
    out_t, grad_t = pl.pallas_call(
        functools.partial(layer_kernel, cfg),
        out_shape=[jax.ShapeDtypeStruct((width, toks), BF)] * 2,
        in_specs=[any_spec] * 4 + [vmem_spec] * 3,
        out_specs=[vmem_spec] * 2,
        scratch_shapes=[
            pltpu.VMEM((per, 2 * width), BF),
            pltpu.VMEM((per, width), BF),
            pltpu.VMEM((pad, dp), F32),
            pltpu.VMEM((2, pad, dp), BF),
            pltpu.VMEM((chunks, pad, cw), BF),
            pltpu.VMEM((dp, dp), BF),
            pltpu.VMEM((dp, dp), BF),
            pltpu.VMEM((chunks, dp, cw), BF),
            pltpu.VMEM((dp, toks), BF),
            pltpu.VMEM((dp, toks), BF),
            pltpu.VMEM((toks, dp), BF),
            pltpu.VMEM(flat, BF),
            pltpu.VMEM(flat, BF),
            pltpu.VMEM(flat, BF),
            pltpu.VMEM(flat, BF),
            pltpu.VMEM(flat, BF),
            pltpu.VMEM(flat, F32),
            pltpu.VMEM(flat, F32),
            pltpu.VMEM(flat, BF),
            pltpu.VMEM(flat, BF),
            pltpu.VMEM((chunks, rows, cw), BF),
            pltpu.VMEM((chunks, rows, cw), BF),
            pltpu.VMEM((chunks, rows, cw), BF),
            pltpu.VMEM((chunks, rows, cw), BF),
            pltpu.VMEM((rows, toks), BF),
            pltpu.VMEM((toks, rows), BF),
            pltpu.VMEM((toks, rows), BF),
            pltpu.VMEM((toks, rows), BF),
            dma((4,)),
            dma((pieces,)),
            dma((pieces,)),
            dma((pieces, 2)),
            dma((pieces, 2, nz // 2)),
            dma((pieces,)),
            dma((pieces,)),
            dma((pieces,)),
            dma((pieces,)),
            dma((2 + 2 * chunks,)),
            dma((2 + 2 * chunks,)),
        ],
        compiler_params=pltpu.CompilerParams(
            collective_id=0, has_side_effects=True, vmem_limit_bytes=60 * 1024 * 1024
        ),
    )(gate_up_weight[0], down_matrix[0], tokens.T, cotangent.T, expert_ids.T, gates.T, jnp.asarray(place))
    return out_t.T, grad_t.T


def solution(mesh):
    in_specs = (
        P(("fsdp", "expert"), None),
        P(("fsdp", "expert"), None),
        P(("fsdp", "expert"), None),
        P(("fsdp", "expert"), None),
        P("expert", "fsdp", None),
        P("expert", "fsdp", None),
    )
    out_specs = (P(("fsdp", "expert"), None), P(("fsdp", "expert"), None))
    return jax.shard_map(
        functools.partial(shards, dict(mesh.shape)), mesh=mesh, in_specs=in_specs, out_specs=out_specs, check_vma=False
    )
```

time: 465 us -> 130 us (0.28)
  waiting for transfers between devices: 313 us -> 0 us
  Pallas kernels: 0 us -> 126 us
  starting transfers between devices: 44.1 us -> 0 us
  local copies, waits for them, and re-layouts: 46.4 us -> 2.96 us
  matrix products: 26.3 us -> 0 us
  other arithmetic: 20.1 us -> 0 us
  between operations: 14.3 us -> 0.65 us
    all_to_all x4 -> x0, waiting for transfers between devices: 210 us -> none  [the longest x1 184 us: shards(): lax.all_to_all(send_rows, 'expert', split_axis=0, concat_axis=0, tiled=True)]
    pallas_call x0 -> x1, Pallas kernels: none -> 126 us  [shards(): pl.pallas_call(functools.partial(layer_kernel, cfg), out_shape=[jax.Shape...]
    all_gather x2 -> x0, waiting for transfers between devices: 103 us -> none  [the longest x1 103 us: shards(): lax.all_gather(down_matrix, 'fsdp', axis=1, tiled=True)]
    all_to_all x4 -> x0, starting transfers between devices: 44 us -> none  [the longest x1 24.4 us: shards(): lax.all_to_all(row_grads, 'expert', split_axis=0, concat_axis=0, tiled=True)]
    dot_general x4 -> x0, matrix products: 26.3 us -> none  [the longest x1 11.2 us: shards(): pre = jnp.dot(rows_in, gate_up_matrix, preferred_element_type=jnp.float32)]
    gather x6 -> x0, local copies, waits for them, and re-layouts: 22.6 us -> none  [the longest x2 11.8 us: shards(): back_rows = grads_flat[places].astype(jnp.float32)]
    reduce_sum x3 -> x0, other arithmetic: 14.2 us -> none  [the longest x1 7.44 us: shards(): output = jnp.sum(gates[:, :, None] * out_rows, axis=1)]
    unnamed x18 -> x4, local copies, waits for them, and re-layouts: 11.9 us -> 2.96 us
  transfers between devices with their start and end apart: 6 -> 0, of which waited for: 5 -> 0; matrix products, arithmetic and copies ran while one was open for 8% -> 0% of each run, Pallas kernels for 0% -> 0%
where the time goes in v1:
time: 130 us
  Pallas kernels  126 us (97%)
  local copies, waits for them, and re-layouts  2.96 us (2%)
    pallas_call x1, Pallas kernels, shards(): pl.pallas_call(functools.partial(layer_kernel, cfg), out_shape=[jax.Shape...  126 us
    unnamed x4, local copies, waits for them, and re-layouts  2.96 us

profile of v1, /device:TPU:1, one launch (start us, length us, event | category | flops | bytes accessed | tf_op | source)
XLA Modules:
  0.0 129.9 jit_solution(17891730603150781775)
XLA Ops:
  0.6 126.3 %shard_map.86 = (bf16[1440,256]{1,0:T(8,128)(2,1)}, bf16[1440,256]{1,0:T(8,128)(2,1)}) custom-call(bf16[45,2880]{1,0:T(8,128)(2,1)} %bitcast.12, bf16[45,1440]{1,0:T(8,128)(2,1)} %bitcast.13, bf16[1440,256]{1,0:T(8,128)(2,1)} %bitcast.8, bf16[1440,256]{1,0:T(8,128)(2,1)} %bitcast.9, s32[4,256]{1,0:T(4,128)} %bitcast.14, f32[4,256]{1,0:T(4,128)} %bitcast.15, ...), custom_call_target="tpu_custom_call" | custom-call | tf_op jit(solution)/shard_map/pallas_call | solution.py:392
  126.9 0.0 copy-start
  127.0 2.1 %copy.11 = bf16[256,1440]{0,1:T(8,128)(2,1)} copy(bf16[256,1440]{0,1:T(8,128)(2,1)} %bitcast.11) | data formatting | bytes 1474560
  129.1 0.0 copy-done
  129.1 0.9 copy.12
Async XLA Ops:
  126.9 2.1 %copy-start = (bf16[1440,256]{1,0:T(8,128)(2,1)S(1)}, bf16[1440,256]{1,0:T(8,128)(2,1)}, u32[]{:S(2)}) copy-start(bf16[1440,256]{1,0:T(8,128)(2,1)} %get-tuple-element.5) | copy-start | bytes 2211844

commit v2 on v1

v2 whole, which is shorter than its diff:
```python
import functools

import jax
import jax.numpy as jnp
import numpy as np
from jax import lax
from jax.experimental import pallas as pl
from jax.experimental.pallas import tpu as pltpu
from jax.sharding import PartitionSpec as P

MESH = pl.DeviceIdType.MESH
CAP = 16
LANE = 128
BF = jnp.bfloat16
F32 = jnp.float32
NN = (((1,), (0,)), ((), ()))
NT = (((1,), (1,)), ((), ()))


def dot(a, b, dims=NN):
    return lax.dot_general(a, b, dims, preferred_element_type=F32)


def onehot(mask):
    return jnp.where(mask, 1.0, 0.0).astype(BF)


def windows(idx, width, cuts):
    edges = [0, *cuts, width]
    found = []
    for lo, hi in zip(edges[:-1], edges[1:]):
        part = idx[(idx >= lo) & (idx < hi)]
        if part.size:
            start = int(part.min()) // LANE * LANE
            found.append((start, min(pl.cdiv(int(part.max()) + 1, LANE) * LANE, hi)))
    return found


def tables(nz, per, pad, width):
    ns = 2 * nz
    dp = ns * pad
    main = per // 8 * 8
    rest = per - main
    head = ns * main
    q = np.arange(width)
    s = np.where(q < head, q // main, (q - head) // rest)
    i = np.where(q < head, q % main, main + (q - head) % rest)
    nat_q, pad_q = per * s + i, pad * s + i
    p = np.arange(dp)
    place = np.where(p % pad < per, per * (p // pad) + p % pad, -1)
    packed_p = np.full(dp, -1)
    packed_p[pad_q] = q
    tail = (width - head) // LANE * LANE
    odd = width - head - tail
    gate_q = np.concatenate([np.arange(head), 2 * head + np.arange(tail), 2 * head + 2 * tail + np.arange(odd)])
    up_q = np.concatenate([head + np.arange(head), 2 * head + tail + np.arange(tail), 2 * head + 2 * tail + odd + np.arange(odd)])
    down_at = 2 * width
    total = pl.cdiv(3 * width, LANE) * LANE
    first = down_at // LANE * LANE
    assert total - first == dp and head % LANE == 0
    own = np.full(total, -1)
    own[gate_q] = nat_q
    own[up_q] = width + nat_q
    from_gate = np.full(total, -1)
    from_gate[gate_q] = pad_q
    from_up = np.full(total, -1)
    from_up[up_q] = pad_q
    table = np.full((8, total), -1, np.int32)
    table[0], table[1, :dp], table[2, :dp], table[3], table[4] = own, place, packed_p, from_gate, from_up
    return dict(head=head, tail=tail, odd=odd, first=first, shift=down_at - first, total=total, dp=dp, table=table)


def layer_kernel(
    cfg,
    gate_up_hbm, down_hbm, tok_hbm, cot_hbm, ids_ref, gates_ref, table_ref,
    out_ref, igrad_ref,
    gu_own, dn_own, own32, own, weights,
    tok, cot, rows_nat, rows_send, rows_in, grads_send, grads_in,
    hid, fac_gate_hi, fac_gate_lo, fac_up_hi, fac_up_lo, hid_pad, fac_gate, fac_up, hid_grad, pg_gate, pg_up, pg,
    out_send, rg_send, out_recv, rg_recv,
    pick, pick_t, mix_hi, mix_lo,
    in_sem, swap_send, swap_recv, ring_send_sem, ring_recv_sem, last_send_sem, last_recv_sem,
    sib_send_sem, sib_recv_sem, a2a_send_sem, a2a_recv_sem, round_sem,
):
    nz, ne, per, pad, width = cfg["nz"], cfg["ne"], cfg["per"], cfg["pad"], cfg["width"]
    head, tail, odd, first, shift = cfg["head"], cfg["tail"], cfg["odd"], cfg["first"], cfg["shift"]
    dp, total, table, pieces = cfg["dp"], cfg["total"], cfg["table"], cfg["pieces"]
    chunks, rows, cw = out_send.shape
    tile = cfg["tile"]
    toks = ids_ref.shape[1]
    kb = nz // 2 - 1

    f = lax.axis_index("fsdp")
    e = lax.axis_index("expert")
    ylo = lax.div(f, nz)
    z = lax.rem(f, nz)
    c = lax.rem(e, 2)
    e2 = lax.div(e, 2)
    keeps = ylo == c
    swaps = ylo != c
    znext = ylo * nz + lax.rem(z + 1, nz)
    zprev = ylo * nz + lax.rem(z + nz - 1, nz)

    bits = ne.bit_length() - 1
    partners = [((1 - ylo) * nz + z, e)]
    for r in range(bits):
        bit = lax.rem(lax.div(e, 2**r), 2)
        partners.append((f, e + (1 - 2 * bit) * 2**r))
    swap_partner = ((1 - ylo) * nz + z, e2 * 2 + 1 - c)
    barrier = pltpu.get_barrier_semaphore()
    near = [(znext, e), (zprev, e), swap_partner] + partners
    for there in near:
        pl.semaphore_signal(barrier, inc=1, device_id=there, device_id_type=MESH)

    def round_signal(r):
        pl.semaphore_signal(round_sem.at[r], inc=1, device_id=partners[r], device_id_type=MESH)

    def round_wait(r):
        pl.semaphore_wait(round_sem.at[r], 1)

    load_gu = pltpu.make_async_copy(gate_up_hbm, gu_own, in_sem.at[0])
    load_dn = pltpu.make_async_copy(down_hbm, dn_own, in_sem.at[1])
    load_tok = pltpu.make_async_copy(tok_hbm, tok.at[pl.ds(0, width)], in_sem.at[2])
    load_cot = pltpu.make_async_copy(cot_hbm, cot.at[pl.ds(shift, width)], in_sem.at[3])
    load_gu.start()
    load_dn.start()
    load_tok.start()
    load_cot.start()

    def pick_columns(src, row, j, cuts=()):
        acc = None
        for start, stop in windows(table[row, LANE * j : LANE * (j + 1)], src.shape[1], cuts):
            col = lax.broadcasted_iota(jnp.int32, (stop - start, LANE), 0) + start
            part = dot(src[:, start:stop], onehot(col == table_ref[row : row + 1, LANE * j : LANE * (j + 1)]))
            acc = part if acc is None else acc + part
        return acc

    own32[...] = jnp.zeros_like(own32)
    load_gu.wait()
    load_dn.wait()
    for j in range(total // LANE):
        part = None
        if (table[0, LANE * j : LANE * (j + 1)] >= 0).any():
            part = pick_columns(gu_own, 0, j, (width // LANE * LANE,))
        lo = max(LANE * j - 2 * width, 0)
        hi = min(LANE * (j + 1) - 2 * width, width)
        if hi > 0:
            start, stop = lo // LANE * LANE, min(pl.cdiv(hi, LANE) * LANE, width)
            col = lax.broadcasted_iota(jnp.int32, (stop - start, LANE), 0) + (start + 2 * width)
            lane = lax.broadcasted_iota(jnp.int32, (stop - start, LANE), 1) + LANE * j
            more = dot(dn_own[:, start:stop], onehot(col == lane))
            part = more if part is None else part + more
        own32[0:per, LANE * j : LANE * (j + 1)] = part
    own[...] = own32[...].astype(BF)

    def piece(p, at, size):
        start, wide = pieces[p]
        return weights.at[pl.ds(pl.multiple_of(at, 16), size), pl.ds(start, wide)]

    def own_piece(p):
        start, wide = pieces[p]
        return own.at[:, pl.ds(start, wide)]

    def block(p, core, b):
        return piece(p, (core * nz + b) * pad, pad)

    def wait_for(ref, sem):
        pltpu.make_async_copy(ref, ref, sem).wait()

    def start_swap(p):
        @pl.when(keeps)
        def _():
            pltpu.make_async_copy(own_piece(p), block(p, c, z), swap_recv.at[p]).start()

        @pl.when(swaps)
        def _():
            pltpu.make_async_remote_copy(
                src_ref=own_piece(p), dst_ref=block(p, 1 - c, z),
                send_sem=swap_send.at[p], recv_sem=swap_recv.at[p],
                device_id=swap_partner, device_id_type=MESH,
            ).start()

    def ring_send(p, way, k):
        b = lax.rem(z + nz - k, nz) if way == 0 else lax.rem(z + k, nz)
        pltpu.make_async_remote_copy(
            src_ref=block(p, c, b), dst_ref=block(p, c, b),
            send_sem=ring_send_sem.at[p, way], recv_sem=ring_recv_sem.at[p, way, k],
            device_id=(znext if way == 0 else zprev, e), device_id_type=MESH,
        ).start()

    def last_send(p):
        b = lax.rem(z + nz - (1 - 2 * c) * kb, nz)
        pltpu.make_async_remote_copy(
            src_ref=block(p, c, b), dst_ref=block(p, c, b),
            send_sem=last_send_sem.at[p], recv_sem=last_recv_sem.at[p],
            device_id=(ylo * nz + lax.rem(z + nz + 1 - 2 * c, nz), e), device_id_type=MESH,
        ).start()

    def sib_send(p, b):
        pltpu.make_async_remote_copy(
            src_ref=block(p, c, b), dst_ref=block(p, c, b),
            send_sem=sib_send_sem.at[p], recv_sem=sib_recv_sem.at[p],
            device_id=(f, e2 * 2 + 1 - c), device_id_type=MESH,
        ).start()

    def ring_open(p):
        wait_for(block(p, c, z), swap_recv.at[p])
        ring_send(p, 0, 0)
        ring_send(p, 1, 0)
        sib_send(p, z)

    def ring_step(p, k):
        came = (lax.rem(z + nz - 1 - k, nz), lax.rem(z + 1 + k, nz))
        for way in range(2):
            wait_for(block(p, c, came[way]), ring_recv_sem.at[p, way, k])
            if k < kb - 1:
                ring_send(p, way, k + 1)
            sib_send(p, came[way])
        if k == kb - 1:
            last_send(p)

    def ring_close(p):
        b = lax.rem(z + nz // 2, nz)
        wait_for(block(p, c, b), last_recv_sem.at[p])
        sib_send(p, b)

    def ring_here(p):
        wait_for(piece(p, (1 - c) * nz * pad, nz * pad), sib_recv_sem.at[p])

    def go(i, src, dst, gf, ge):
        @pl.when((gf != f) | (ge != e))
        def _():
            pltpu.make_async_remote_copy(
                src_ref=src, dst_ref=dst, send_sem=a2a_send_sem.at[i], recv_sem=a2a_recv_sem.at[i],
                device_id=(gf, ge), device_id_type=MESH,
            ).start()

        @pl.when((gf == f) & (ge == e))
        def _():
            pltpu.make_async_copy(src, dst, a2a_recv_sem.at[i]).start()

    def sixteen(ref, i):
        return ref.at[pl.ds(pl.multiple_of(i * CAP, CAP), CAP)]

    def send_out(i, src, dst):
        def one(t, _):
            x = lax.rem(e + t, ne)
            go(i, sixteen(src, x), sixteen(dst, e), lax.rem(x, 2) * nz + z, lax.div(x, 2) * 2 + ylo)
            return 0

        lax.fori_loop(0, ne, one, 0)

    def send_back(i, src, dst):
        def one(t, _):
            x = lax.rem(e + ne // 2 + lax.div(t, 2) * (1 - 2 * lax.rem(t, 2)) - lax.rem(t, 2) + ne, ne)
            go(i, sixteen(src, x), sixteen(dst, e2 * 2 + ylo), c * nz + z, x)
            return 0

        lax.fori_loop(0, ne, one, 0)

    def sent(i, src):
        @pl.when(keeps)
        def _():
            wait_for(src.at[pl.ds(0, rows - CAP)], a2a_send_sem.at[i])

        @pl.when(swaps)
        def _():
            wait_for(src, a2a_send_sem.at[i])

    def make_slots():
        ci = lax.broadcasted_iota(jnp.int32, (rows, toks), 0)
        expert = lax.shift_right_logical(ci, 4)
        hit = jnp.zeros((rows, toks), F32)
        gate = jnp.zeros((rows, toks), F32)
        for k in range(ids_ref.shape[0]):
            same = ids_ref[k : k + 1, :] == expert
            hit = jnp.where(same, 1.0, hit)
            gate = jnp.where(same, gates_ref[k : k + 1, :], gate)
        earlier = onehot(
            lax.broadcasted_iota(jnp.int32, (toks, toks), 0) < lax.broadcasted_iota(jnp.int32, (toks, toks), 1)
        )
        slot = dot(hit.astype(BF), earlier)
        want = jnp.bitwise_and(ci, CAP - 1).astype(F32)
        kept = jnp.where(slot == want, hit, 0.0)
        gate = gate * kept
        pick[...] = kept.astype(BF)
        pick_t[...] = kept.T.astype(BF)
        mixed = gate.T
        high = mixed.astype(BF)
        mix_hi[...] = high
        mix_lo[...] = (mixed - high.astype(F32)).astype(BF)
        return jnp.sum(gate, axis=1, keepdims=True)

    def columns(n, base=0):
        return slice(base + tile * n, base + tile * (n + 1))

    def lanes(j):
        return slice(LANE * j, LANE * (j + 1))

    def make_rows():
        load_tok.wait()
        for n in range(dp // tile):
            rows_nat[:, columns(n)] = dot(pick[...], tok[columns(n), :], NT).astype(BF)
        for j in range(dp // LANE):
            rows_send[:, lanes(j)] = pick_columns(rows_nat, 1, j).astype(BF)

    def make_grads(slot_gate):
        load_cot.wait()
        for n in range(dp // tile):
            grads_send[:, columns(n)] = (dot(pick[...], cot[columns(n), :], NT) * slot_gate).astype(BF)

    def activate(at, act, upper):
        here = slice(at, at + act.shape[1])
        sigma = jax.nn.sigmoid(act)
        gated = act * sigma
        hid[:, here] = (gated * upper).astype(BF)
        slope = upper * sigma * (1.0 + act * (1.0 - sigma))
        for value, high_ref, low_ref in ((slope, fac_gate_hi, fac_gate_lo), (gated, fac_up_hi, fac_up_lo)):
            high = value.astype(BF)
            high_ref[:, here] = high
            low_ref[:, here] = (value - high.astype(F32)).astype(BF)

    def forward_main(n):
        activate(
            tile * n, dot(rows_in[...], weights[:, columns(n)]), dot(rows_in[...], weights[:, columns(n, head)])
        )

    def forward_rest():
        at = 2 * head
        if tail:
            both = dot(rows_in[...], weights[:, at : at + 2 * tail])
            activate(head, both[:, 0:tail], both[:, tail : 2 * tail])
        both = dot(rows_in[...], weights[:, at + 2 * tail : at + 2 * tail + LANE])
        activate(head + tail, both, pltpu.roll(both, LANE - odd, 1))

    def spread(j):
        hid_pad[:, lanes(j)] = pick_columns(hid, 2, j, (head,)).astype(BF)
        fac_gate[:, lanes(j)] = pick_columns(fac_gate_hi, 2, j, (head,)) + pick_columns(fac_gate_lo, 2, j, (head,))
        fac_up[:, lanes(j)] = pick_columns(fac_up_hi, 2, j, (head,)) + pick_columns(fac_up_lo, 2, j, (head,))

    def send_result(n):
        out_send[n] = dot(hid_pad[...], weights[:, first + cw * n : first + cw * (n + 1)]).astype(BF)
        send_back(2 + n, out_send.at[n], out_recv.at[n])

    def backward_part(m, n):
        part = dot(grads_in[:, cw * m : cw * (m + 1)], weights[columns(n), first + cw * m : first + cw * (m + 1)], NT)
        if m > 0:
            part = part + hid_grad[:, columns(n)]
        if m < chunks - 1:
            hid_grad[:, columns(n)] = part
        else:
            pg_gate[:, columns(n)] = (part * fac_gate[:, columns(n)]).astype(BF)
            pg_up[:, columns(n)] = (part * fac_up[:, columns(n)]).astype(BF)

    def pack(j):
        part = None
        for row, src in ((3, pg_gate), (4, pg_up)):
            if (table[row, lanes(j)] >= 0).any():
                more = pick_columns(src, row, j)
                part = more if part is None else part + more
        pg[:, lanes(j)] = part.astype(BF)

    tok[width:dp, :] = jnp.zeros((dp - width, toks), BF)
    cot[0:shift, :] = jnp.zeros((shift, toks), BF)
    cot[shift + width : dp, :] = jnp.zeros((dp - shift - width, toks), BF)
    hid[:, width:dp] = jnp.zeros((rows, dp - width), BF)

    pl.semaphore_wait(barrier, len(near))

    count = len(pieces)
    offsets = cfg["offsets"]
    for p in range(count):
        start_swap(p)
    events = []
    for p in range(count):
        events.append((offsets[p] - 1, 0, p, -1))
        events += [(offsets[p] + k, 1, p, k) for k in range(kb)]
        events.append((offsets[p] + kb, 2, p, kb))
    events.sort()
    work = []

    def run(n):
        for _ in range(min(n, len(work))):
            work.pop(0)()

    held = {}

    def prepare_rows():
        held["gate"] = make_slots()
        make_rows()

    def launch_rows():
        send_out(0, rows_send, rows_in)

    def launch_grads():
        make_grads(held["gate"])
        send_out(1, grads_send, grads_in)

    needed = cfg["needed"]
    tiles = dp // tile
    visits = {(r % needed, r // needed): r for r in range(bits + 1)}
    launch = ((bits + 1) % needed, (bits + 1) // needed)
    ended = set()
    round_signal(0)
    for _, _, p, k in events:
        if k == kb and p >= needed:
            run(len(work))
        if k < 0:
            ring_open(p)
        elif k < kb:
            ring_step(p, k)
        else:
            ring_close(p)
            ended.add(p)
        if (p, k) in visits:
            r = visits[p, k]
            round_wait(r)
            if r < bits:
                round_signal(r + 1)
        if (p, k) == (needed - 1, 0):
            prepare_rows()
        if (p, k) == launch:
            launch_rows()
        if (p, k) == (launch[0], launch[1] + 1):
            launch_grads()
        if k == kb and p == needed - 1:
            for q in range(needed):
                ring_here(q)
            wait_for(rows_in, a2a_recv_sem.at[0])
            work += [functools.partial(forward_main, n) for n in range(head // tile)] + [forward_rest]
            work += [functools.partial(spread, j) for j in range(dp // LANE)]
            work += [functools.partial(send_result, 0)]
            work += [functools.partial(wait_for, grads_in, a2a_recv_sem.at[1])]
            work += [functools.partial(backward_part, 0, n) for n in range(tiles)]
        elif ended >= set(range(needed)) and k < kb and p == count - 1:
            run(4)
        if k == kb and p >= needed:
            n = p - needed + 1
            ring_here(p)
            send_result(n)
            for m in range(tiles):
                backward_part(n, m)
    for j in range(pl.cdiv(2 * width, LANE)):
        pack(j)
    wide = pl.cdiv(2 * width, LANE) * LANE
    for n in range(chunks):
        for m in range(cw // tile):
            here = slice(cw * n + tile * m, cw * n + tile * (m + 1))
            rg_send[n, :, columns(m)] = dot(pg[...], weights[here, 0:wide], NT).astype(BF)
        send_back(2 + chunks + n, rg_send.at[n], rg_recv.at[n])

    eye = onehot(
        lax.broadcasted_iota(jnp.int32, (LANE, LANE), 0) == lax.broadcasted_iota(jnp.int32, (LANE, LANE), 1)
    )
    for n in range(chunks):
        wait_for(out_recv.at[n], a2a_recv_sem.at[2 + n])
        summed = (dot(mix_hi[...], out_recv[n]) + dot(mix_lo[...], out_recv[n])).astype(BF)
        for m in range(cw // LANE):
            d = cw * n + LANE * m - shift
            lo, hi = max(d, 0), min(d + LANE, width)
            if hi > lo:
                turned = dot(eye, summed[:, lanes(m)], NT).astype(BF)
                out_ref[lo:hi, :] = turned[lo - d : hi - d, :]
    for n in range(chunks):
        wait_for(rg_recv.at[n], a2a_recv_sem.at[2 + chunks + n])
        rows_nat[:, cw * n : cw * (n + 1)] = dot(pick_t[...], rg_recv[n]).astype(BF)
    for j in range(pl.cdiv(width, LANE)):
        d = np.arange(LANE * j, min(width, LANE * (j + 1)))
        p = pad * (d // per) + d % per
        start = int(p.min()) // LANE * LANE
        stop = (int(p.max()) // LANE + 1) * LANE
        di = lax.broadcasted_iota(jnp.int32, (LANE, stop - start), 0) + LANE * j
        sel = onehot(di == table_ref[1:2, start:stop])
        turned = dot(sel, rows_nat[:, start:stop], NT).astype(BF)
        igrad_ref[LANE * j : LANE * j + len(d), :] = turned[0 : len(d), :]

    for p in range(count):
        for way in range(2):
            wait_for(piece(p, 0, kb * pad), ring_send_sem.at[p, way])
        wait_for(piece(p, 0, pad), last_send_sem.at[p])
        wait_for(piece(p, 0, nz * pad), sib_send_sem.at[p])

        @pl.when(swaps)
        def _():
            wait_for(own_piece(p), swap_send.at[p])

    sent(0, rows_send)
    sent(1, grads_send)
    for n in range(chunks):
        sent(2 + n, out_send.at[n])
        sent(2 + chunks + n, rg_send.at[n])


def shards(mesh_shape, tokens, cotangent, expert_ids, gates, gate_up_weight, down_matrix):
    ne = mesh_shape["expert"]
    nz = mesh_shape["fsdp"] // 2
    toks, width = tokens.shape
    per = down_matrix.shape[1]
    pad = pl.cdiv(per, 16) * 16
    cfg = tables(nz, per, pad, width)
    dp, total, head, first = cfg["dp"], cfg["total"], cfg["head"], cfg["first"]
    chunks = 3
    cw = dp // chunks
    tile = 256 if cw % 256 == 0 and head % 256 == 0 else 128
    rows = ne * CAP
    pieces = [(0, head), (head, head), (2 * head, first + cw - 2 * head), (first + cw, cw), (first + 2 * cw, cw)]
    cfg.update(nz=nz, ne=ne, per=per, pad=pad, width=width, tile=tile, pieces=pieces, needed=3, offsets=(0, 0, 0, 1, 1))
    any_spec = pl.BlockSpec(memory_space=pl.ANY)
    vmem_spec = pl.BlockSpec(memory_space=pltpu.VMEM)
    dma = pltpu.SemaphoreType.DMA
    flat = (rows, dp)
    wide = pl.cdiv(2 * width, LANE) * LANE
    count = len(pieces)
    out_t, grad_t = pl.pallas_call(
        functools.partial(layer_kernel, cfg),
        out_shape=[jax.ShapeDtypeStruct((width, toks), BF)] * 2,
        in_specs=[any_spec] * 4 + [vmem_spec] * 3,
        out_specs=[vmem_spec] * 2,
        scratch_shapes=[
            pltpu.VMEM((per, 2 * width), BF),
            pltpu.VMEM((per, width), BF),
            pltpu.VMEM((pad, total), F32),
            pltpu.VMEM((pad, total), BF),
            pltpu.VMEM((dp, total), BF),
            pltpu.VMEM((dp, toks), BF),
            pltpu.VMEM((dp, toks), BF),
            pltpu.VMEM((toks, dp), BF),
        ]
        + [pltpu.VMEM(flat, BF)] * 10
        + [pltpu.VMEM(flat, F32)] * 3
        + [pltpu.VMEM(flat, BF)] * 2
        + [pltpu.VMEM((rows, wide), BF)]
        + [pltpu.VMEM((chunks, rows, cw), BF)] * 4
        + [
            pltpu.VMEM((rows, toks), BF),
            pltpu.VMEM((toks, rows), BF),
            pltpu.VMEM((toks, rows), BF),
            pltpu.VMEM((toks, rows), BF),
            dma((4,)),
            dma((count,)),
            dma((count,)),
            dma((count, 2)),
            dma((count, 2, nz // 2)),
            dma((count,)),
            dma((count,)),
            dma((count,)),
            dma((count,)),
            dma((2 + 2 * chunks,)),
            dma((2 + 2 * chunks,)),
            pltpu.SemaphoreType.REGULAR((ne.bit_length(),)),
        ],
        compiler_params=pltpu.CompilerParams(
            collective_id=0, has_side_effects=True, vmem_limit_bytes=60 * 1024 * 1024
        ),
    )(gate_up_weight[0], down_matrix[0], tokens.T, cotangent.T, expert_ids.T, gates.T, jnp.asarray(cfg["table"]))
    return out_t.T, grad_t.T


def solution(mesh):
    in_specs = (
        P(("fsdp", "expert"), None),
        P(("fsdp", "expert"), None),
        P(("fsdp", "expert"), None),
        P(("fsdp", "expert"), None),
        P("expert", "fsdp", None),
        P("expert", "fsdp", None),
    )
    out_specs = (P(("fsdp", "expert"), None), P(("fsdp", "expert"), None))
    return jax.shard_map(
        functools.partial(shards, dict(mesh.shape)), mesh=mesh, in_specs=in_specs, out_specs=out_specs, check_vma=False
    )
```

time: 130 us -> 119 us (0.915)
  Pallas kernels: 126 us -> 115 us
    pallas_call x1, Pallas kernels: 126 us -> 115 us  [shards(): pl.pallas_call(functools.partial(layer_kernel, cfg), out_shape=[jax.Shape...]
where the time goes in v2:
time: 119 us; the launch traced here: 118 us
  Pallas kernels  115 us (97%)
  local copies, waits for them, and re-layouts  2.96 us (2%)
    pallas_call x1, Pallas kernels, shards(): pl.pallas_call(functools.partial(layer_kernel, cfg), out_shape=[jax.Shape...  115 us
    unnamed x4, local copies, waits for them, and re-layouts  2.96 us

profile of v2, /device:TPU:1, one launch (start us, length us, event | category | flops | bytes accessed | tf_op | source)
XLA Modules:
  0.0 118.5 jit_solution(10022603297302758556)
XLA Ops:
  0.6 114.9 %shard_map.86 = (bf16[1440,256]{1,0:T(8,128)(2,1)}, bf16[1440,256]{1,0:T(8,128)(2,1)}) custom-call(bf16[45,2880]{1,0:T(8,128)(2,1)} %bitcast.12, bf16[45,1440]{1,0:T(8,128)(2,1)} %bitcast.13, bf16[1440,256]{1,0:T(8,128)(2,1)} %bitcast.10, bf16[1440,256]{1,0:T(8,128)(2,1)} %bitcast.11, s32[4,256]{1,0:T(4,128)} %bitcast.14, f32[4,256]{1,0:T(4,128)} %bitcast.15, ...), custom_call_target="tpu_custom_call" | custom-call | tf_op jit(solution)/shard_map/pallas_call | solution.py:514
  115.5 0.0 copy-start
  115.5 2.1 %copy.11 = bf16[256,1440]{0,1:T(8,128)(2,1)} copy(bf16[256,1440]{0,1:T(8,128)(2,1)} %bitcast.9) | data formatting | bytes 1474560
  117.6 0.0 copy-done
  117.6 0.9 copy.12
Async XLA Ops:
  115.5 2.1 %copy-start = (bf16[1440,256]{1,0:T(8,128)(2,1)S(1)}, bf16[1440,256]{1,0:T(8,128)(2,1)}, u32[]{:S(2)}) copy-start(bf16[1440,256]{1,0:T(8,128)(2,1)} %get-tuple-element.5) | copy-start | bytes 2211844

commit v3 on v2

--- a/solution.py
+++ b/solution.py
@@ -127,11 +127,11 @@
     load_tok.start()
     load_cot.start()
 
-    def pick_columns(src, row, j, cuts=()):
+    def pick_columns(src, row, j, cuts=(), size=LANE):
         acc = None
-        for start, stop in windows(table[row, LANE * j : LANE * (j + 1)], src.shape[1], cuts):
-            col = lax.broadcasted_iota(jnp.int32, (stop - start, LANE), 0) + start
-            part = dot(src[:, start:stop], onehot(col == table_ref[row : row + 1, LANE * j : LANE * (j + 1)]))
+        for start, stop in windows(table[row, size * j : size * (j + 1)], src.shape[1], cuts):
+            col = lax.broadcasted_iota(jnp.int32, (stop - start, size), 0) + start
+            part = dot(src[:, start:stop], onehot(col == table_ref[row : row + 1, size * j : size * (j + 1)]))
             acc = part if acc is None else acc + part
         return acc
 
@@ -334,9 +334,10 @@
         activate(head + tail, both, pltpu.roll(both, LANE - odd, 1))
 
     def spread(j):
-        hid_pad[:, lanes(j)] = pick_columns(hid, 2, j, (head,)).astype(BF)
-        fac_gate[:, lanes(j)] = pick_columns(fac_gate_hi, 2, j, (head,)) + pick_columns(fac_gate_lo, 2, j, (head,))
-        fac_up[:, lanes(j)] = pick_columns(fac_up_hi, 2, j, (head,)) + pick_columns(fac_up_lo, 2, j, (head,))
+        here = columns(j)
+        hid_pad[:, here] = pick_columns(hid, 2, j, (head,), tile).astype(BF)
+        fac_gate[:, here] = pick_columns(fac_gate_hi, 2, j, (head,), tile) + pick_columns(fac_gate_lo, 2, j, (head,), tile)
+        fac_up[:, here] = pick_columns(fac_up_hi, 2, j, (head,), tile) + pick_columns(fac_up_lo, 2, j, (head,), tile)
 
     def send_result(n):
         out_send[n] = dot(hid_pad[...], weights[:, first + cw * n : first + cw * (n + 1)]).astype(BF)
@@ -352,13 +353,14 @@
             pg_gate[:, columns(n)] = (part * fac_gate[:, columns(n)]).astype(BF)
             pg_up[:, columns(n)] = (part * fac_up[:, columns(n)]).astype(BF)
 
-    def pack(j):
+    def pack(j, size):
         part = None
+        here = slice(size * j, size * (j + 1))
         for row, src in ((3, pg_gate), (4, pg_up)):
-            if (table[row, lanes(j)] >= 0).any():
-                more = pick_columns(src, row, j)
+            if (table[row, here] >= 0).any():
+                more = pick_columns(src, row, j, (), size)
                 part = more if part is None else part + more
-        pg[:, lanes(j)] = part.astype(BF)
+        pg[:, here] = part.astype(BF)
 
     tok[width:dp, :] = jnp.zeros((dp - width, toks), BF)
     cot[0:shift, :] = jnp.zeros((shift, toks), BF)
@@ -398,8 +400,7 @@
 
     needed = cfg["needed"]
     tiles = dp // tile
-    visits = {(r % needed, r // needed): r for r in range(bits + 1)}
-    launch = ((bits + 1) % needed, (bits + 1) // needed)
+    steps = 0
     ended = set()
     round_signal(0)
     for _, _, p, k in events:
@@ -412,36 +413,42 @@
         else:
             ring_close(p)
             ended.add(p)
-        if (p, k) in visits:
-            r = visits[p, k]
-            round_wait(r)
-            if r < bits:
-                round_signal(r + 1)
-        if (p, k) == (needed - 1, 0):
-            prepare_rows()
-        if (p, k) == launch:
-            launch_rows()
-        if (p, k) == (launch[0], launch[1] + 1):
-            launch_grads()
-        if k == kb and p == needed - 1:
-            for q in range(needed):
+        if 0 <= k < kb:
+            if steps <= bits:
+                round_wait(steps)
+                if steps < bits:
+                    round_signal(steps + 1)
+            if steps == 2:
+                prepare_rows()
+            if steps == bits + 1:
+                launch_rows()
+            if steps == bits + 3:
+                launch_grads()
+            steps += 1
+        if k == kb and p == needed - 2:
+            for q in range(needed - 1):
                 ring_here(q)
             wait_for(rows_in, a2a_recv_sem.at[0])
-            work += [functools.partial(forward_main, n) for n in range(head // tile)] + [forward_rest]
-            work += [functools.partial(spread, j) for j in range(dp // LANE)]
+            work += [functools.partial(forward_main, n) for n in range(head // tile)]
+        elif k == kb and p == needed - 1:
+            run(len(work))
+            ring_here(p)
+            work += [forward_rest] + [functools.partial(spread, j) for j in range(tiles)]
             work += [functools.partial(send_result, 0)]
             work += [functools.partial(wait_for, grads_in, a2a_recv_sem.at[1])]
             work += [functools.partial(backward_part, 0, n) for n in range(tiles)]
-        elif ended >= set(range(needed)) and k < kb and p == count - 1:
-            run(4)
+        elif p >= min(needed - 1, count - 1) and k < kb:
+            run(cfg["burst"])
         if k == kb and p >= needed:
             n = p - needed + 1
             ring_here(p)
             send_result(n)
             for m in range(tiles):
                 backward_part(n, m)
-    for j in range(pl.cdiv(2 * width, LANE)):
-        pack(j)
+    for j in range(2 * head // tile):
+        pack(j, tile)
+    for j in range(2 * head // LANE, pl.cdiv(2 * width, LANE)):
+        pack(j, LANE)
     wide = pl.cdiv(2 * width, LANE) * LANE
     for n in range(chunks):
         for m in range(cw // tile):
@@ -504,7 +511,7 @@
     tile = 256 if cw % 256 == 0 and head % 256 == 0 else 128
     rows = ne * CAP
     pieces = [(0, head), (head, head), (2 * head, first + cw - 2 * head), (first + cw, cw), (first + 2 * cw, cw)]
-    cfg.update(nz=nz, ne=ne, per=per, pad=pad, width=width, tile=tile, pieces=pieces, needed=3, offsets=(0, 0, 0, 1, 1))
+    cfg.update(nz=nz, ne=ne, per=per, pad=pad, width=width, tile=tile, pieces=pieces, needed=3, offsets=(0, 0, 1, 3, 3), burst=1)
     any_spec = pl.BlockSpec(memory_space=pl.ANY)
     vmem_spec = pl.BlockSpec(memory_space=pltpu.VMEM)
     dma = pltpu.SemaphoreType.DMA
@@ -513,7 +520,7 @@
     count = len(pieces)
     out_t, grad_t = pl.pallas_call(
         functools.partial(layer_kernel, cfg),
-        out_shape=[jax.ShapeDtypeStruct((width, toks), BF)] * 2,
+        out_shape=[pltpu.VMEM((width, toks), BF)] * 2,
         in_specs=[any_spec] * 4 + [vmem_spec] * 3,
         out_specs=[vmem_spec] * 2,
         scratch_shapes=[

time: 119 us -> 115 us (0.966)
  Pallas kernels: 115 us -> 112 us
  local copies, waits for them, and re-layouts: 2.96 us -> 1.73 us
    pallas_call x1, Pallas kernels: 115 us -> 112 us  [shards(): pl.pallas_call(functools.partial(layer_kernel, cfg), out_shape=[pltpu.VME...]
    unnamed x4 -> x2, local copies, waits for them, and re-layouts: 2.96 us -> 1.73 us
where the time goes in v3:
time: 115 us
  Pallas kernels  112 us (97%)
  local copies, waits for them, and re-layouts  1.73 us (2%)
    pallas_call x1, Pallas kernels, shards(): pl.pallas_call(functools.partial(layer_kernel, cfg), out_shape=[pltpu.VME...  112 us

profile of v3, /device:TPU:1, one launch (start us, length us, event | category | flops | bytes accessed | tf_op | source)
XLA Modules:
  0.0 114.6 jit_solution(13317120990549372816)
XLA Ops:
  0.6 112.2 %shard_map.86 = (bf16[1440,256]{1,0:T(8,128)(2,1)S(1)}, bf16[1440,256]{1,0:T(8,128)(2,1)S(1)}) custom-call(bf16[45,2880]{1,0:T(8,128)(2,1)} %bitcast.12, bf16[45,1440]{1,0:T(8,128)(2,1)} %bitcast.13, bf16[1440,256]{1,0:T(8,128)(2,1)} %bitcast.10, bf16[1440,256]{1,0:T(8,128)(2,1)} %bitcast.11, s32[4,256]{1,0:T(4,128)} %bitcast.14, f32[4,256]{1,0:T(4,128)} %bitcast.15, ...), custom_call_target="tpu_custom_call" | custom-call | tf_op jit(solution)/shard_map/pallas_call | solution.py:521
  112.8 0.9 copy.11
  113.7 0.9 copy.12

commit v4 on v3

--- a/solution.py
+++ b/solution.py
@@ -227,36 +227,46 @@
     def ring_here(p):
         wait_for(piece(p, (1 - c) * nz * pad, nz * pad), sib_recv_sem.at[p])
 
-    def go(i, src, dst, gf, ge):
-        @pl.when((gf != f) | (ge != e))
-        def _():
-            pltpu.make_async_remote_copy(
-                src_ref=src, dst_ref=dst, send_sem=a2a_send_sem.at[i], recv_sem=a2a_recv_sem.at[i],
-                device_id=(gf, ge), device_id_type=MESH,
-            ).start()
-
-        @pl.when((gf == f) & (ge == e))
+    def far(i, src, dst, gf, ge):
+        pltpu.make_async_remote_copy(
+            src_ref=src, dst_ref=dst, send_sem=a2a_send_sem.at[i], recv_sem=a2a_recv_sem.at[i],
+            device_id=(gf, ge), device_id_type=MESH,
+        ).start()
+
+    def same_place(i, src, dst, gf, ge):
+        @pl.when(swaps)
+        def _():
+            far(i, src, dst, gf, ge)
+
+        @pl.when(keeps)
         def _():
             pltpu.make_async_copy(src, dst, a2a_recv_sem.at[i]).start()
+
+    def others(send):
+        def one(t, _):
+            x = e + jnp.where(t < ne // 2, t + ne // 2, ne - 1 - t)
+            send(jnp.where(x >= ne, x - ne, x))
+            return 0
+
+        lax.fori_loop(0, ne - 1, one, 0)
 
     def sixteen(ref, i):
         return ref.at[pl.ds(pl.multiple_of(i * CAP, CAP), CAP)]
 
     def send_out(i, src, dst):
-        def one(t, _):
-            x = lax.rem(e + t, ne)
-            go(i, sixteen(src, x), sixteen(dst, e), lax.rem(x, 2) * nz + z, lax.div(x, 2) * 2 + ylo)
-            return 0
-
-        lax.fori_loop(0, ne, one, 0)
+        def send(x, put=far):
+            odd_x = lax.rem(x, 2)
+            put(i, sixteen(src, x), sixteen(dst, e), odd_x * nz + z, x - odd_x + ylo)
+
+        others(send)
+        send(e, same_place)
 
     def send_back(i, src, dst):
-        def one(t, _):
-            x = lax.rem(e + ne // 2 + lax.div(t, 2) * (1 - 2 * lax.rem(t, 2)) - lax.rem(t, 2) + ne, ne)
-            go(i, sixteen(src, x), sixteen(dst, e2 * 2 + ylo), c * nz + z, x)
-            return 0
-
-        lax.fori_loop(0, ne, one, 0)
+        def send(x, put=far):
+            put(i, sixteen(src, x), sixteen(dst, e2 * 2 + ylo), c * nz + z, x)
+
+        others(send)
+        send(e, same_place)
 
     def sent(i, src):
         @pl.when(keeps)
@@ -468,18 +478,22 @@
             if hi > lo:
                 turned = dot(eye, summed[:, lanes(m)], NT).astype(BF)
                 out_ref[lo:hi, :] = turned[lo - d : hi - d, :]
+    turned_tiles = 0
     for n in range(chunks):
         wait_for(rg_recv.at[n], a2a_recv_sem.at[2 + chunks + n])
         rows_nat[:, cw * n : cw * (n + 1)] = dot(pick_t[...], rg_recv[n]).astype(BF)
-    for j in range(pl.cdiv(width, LANE)):
-        d = np.arange(LANE * j, min(width, LANE * (j + 1)))
-        p = pad * (d // per) + d % per
-        start = int(p.min()) // LANE * LANE
-        stop = (int(p.max()) // LANE + 1) * LANE
-        di = lax.broadcasted_iota(jnp.int32, (LANE, stop - start), 0) + LANE * j
-        sel = onehot(di == table_ref[1:2, start:stop])
-        turned = dot(sel, rows_nat[:, start:stop], NT).astype(BF)
-        igrad_ref[LANE * j : LANE * j + len(d), :] = turned[0 : len(d), :]
+        for j in range(turned_tiles, pl.cdiv(width, LANE)):
+            d = np.arange(LANE * j, min(width, LANE * (j + 1)))
+            p = pad * (d // per) + d % per
+            start = int(p.min()) // LANE * LANE
+            stop = (int(p.max()) // LANE + 1) * LANE
+            if stop > cw * (n + 1):
+                break
+            turned_tiles = j + 1
+            di = lax.broadcasted_iota(jnp.int32, (LANE, stop - start), 0) + LANE * j
+            sel = onehot(di == table_ref[1:2, start:stop])
+            turned = dot(sel, rows_nat[:, start:stop], NT).astype(BF)
+            igrad_ref[LANE * j : LANE * j + len(d), :] = turned[0 : len(d), :]
 
     for p in range(count):
         for way in range(2):

time: 115 us -> 114 us (level)
  no operation moved by 1% of the time
where the time goes in v4:
time: 114 us
  Pallas kernels  111 us (97%)
  local copies, waits for them, and re-layouts  1.73 us (2%)
    pallas_call x1, Pallas kernels, shards(): pl.pallas_call(functools.partial(layer_kernel, cfg), out_shape=[pltpu.VME...  111 us

profile of v4, /device:TPU:1, one launch (start us, length us, event | category | flops | bytes accessed | tf_op | source)
XLA Modules:
  0.0 113.8 jit_solution(3443665933862950370)
XLA Ops:
  0.6 111.4 %shard_map.86 = (bf16[1440,256]{1,0:T(8,128)(2,1)S(1)}, bf16[1440,256]{1,0:T(8,128)(2,1)S(1)}) custom-call(bf16[45,2880]{1,0:T(8,128)(2,1)} %bitcast.12, bf16[45,1440]{1,0:T(8,128)(2,1)} %bitcast.13, bf16[1440,256]{1,0:T(8,128)(2,1)} %bitcast.10, bf16[1440,256]{1,0:T(8,128)(2,1)} %bitcast.11, s32[4,256]{1,0:T(4,128)} %bitcast.14, f32[4,256]{1,0:T(4,128)} %bitcast.15, ...), custom_call_target="tpu_custom_call" | custom-call | tf_op jit(solution)/shard_map/pallas_call | solution.py:535
  112.0 0.9 copy.11
  112.9 0.9 copy.12

commit v5 on v4

--- a/solution.py
+++ b/solution.py
@@ -412,6 +412,7 @@
     tiles = dp // tile
     steps = 0
     ended = set()
+    late = []
     round_signal(0)
     for _, _, p, k in events:
         if k == kb and p >= needed:
@@ -423,6 +424,8 @@
         else:
             ring_close(p)
             ended.add(p)
+            while late:
+                late.pop(0)()
         if 0 <= k < kb:
             if steps <= bits:
                 round_wait(steps)
@@ -454,7 +457,10 @@
             ring_here(p)
             send_result(n)
             for m in range(tiles):
-                backward_part(n, m)
+                if n < chunks - 1:
+                    late.append(functools.partial(backward_part, n, m))
+                else:
+                    backward_part(n, m)
     for j in range(2 * head // tile):
         pack(j, tile)
     for j in range(2 * head // LANE, pl.cdiv(2 * width, LANE)):

time: 114 us -> 114 us (level)
  no operation moved by 1% of the time
where the time goes in v5:
time: 114 us
  Pallas kernels  111 us (97%)
  local copies, waits for them, and re-layouts  1.73 us (2%)
    pallas_call x1, Pallas kernels, shards(): pl.pallas_call(functools.partial(layer_kernel, cfg), out_shape=[pltpu.VME...  111 us

profile of v5, /device:TPU:1, one launch (start us, length us, event | category | flops | bytes accessed | tf_op | source)
XLA Modules:
  0.0 113.8 jit_solution(13001740213882946161)
XLA Ops:
  0.6 111.4 %shard_map.86 = (bf16[1440,256]{1,0:T(8,128)(2,1)S(1)}, bf16[1440,256]{1,0:T(8,128)(2,1)S(1)}) custom-call(bf16[45,2880]{1,0:T(8,128)(2,1)} %bitcast.12, bf16[45,1440]{1,0:T(8,128)(2,1)} %bitcast.13, bf16[1440,256]{1,0:T(8,128)(2,1)} %bitcast.10, bf16[1440,256]{1,0:T(8,128)(2,1)} %bitcast.11, s32[4,256]{1,0:T(4,128)} %bitcast.14, f32[4,256]{1,0:T(4,128)} %bitcast.15, ...), custom_call_target="tpu_custom_call" | custom-call | tf_op jit(solution)/shard_map/pallas_call | solution.py:541
  112.0 0.9 copy.11
  112.9 0.9 copy.12
